TPU v7x, 512 devices: a whole 4x4x16 slice. The times are simulated.
512 devices in a mesh: replica: 64 (over x_lo, z, core), tensor: 8 (over x_hi, y).
Axes of the slice: x: 4 (x_hi: 2, x_lo: 2; x = x_hi * 2 + x_lo), y: 4, z: 16, core: 2. Of those that a mesh axis runs over, the one named last changes fastest.
Arguments:
- qkv_weight: bfloat16 [5120, 7168], P(('replica', 'tensor')), may hold values from -0.078125 to 0.078125
- qkv_bias: bfloat16 [7168], P('tensor'), may hold values from -7 to 7
- norm_gain: bfloat16 [5120], replicated, may hold values from 0.099609375 to 1.8984375
- decode_hidden: bfloat16 [1024, 5120], P('replica'), may hold values from -6 to 6
- stored_keys: bfloat16 [1024, 8, 256, 128], P('replica', 'tensor'), may hold values from -72 to 72
- stored_values: bfloat16 [1024, 8, 256, 128], P('replica', 'tensor'), may hold values from -6 to 6
- stored_lengths: int32 [64, 16], P('replica'), may hold values from 1 to 256, 2048 in all within a row
- response_hidden: bfloat16 [640, 64, 5120], P('replica', None, 'tensor'), may hold values from -6 to 6
- response_lengths: int32 [64, 10], P('replica'), may hold values from 1 to 64, 560 in all within a row
- response_target: int32 [640, 1], P('replica'), may hold values from 0 to 7; in each aligned block of 10 rows (0 to 9, 10 to 19, ...) at most 2 rows name the same one
Outputs:
- step_attention: bfloat16 [1024, 5120], P('replica', 'tensor')
- learner_attention: bfloat16 [1024, 64, 5120], P(('replica', 'tensor'))
Inputs may be any that keep to these rules, and one draw needn't show every extreme that they name: `response_lengths`: the 10 lengths of one group sum to 560, and one of them equals 64. `stored_lengths`: the 16 lengths of one group sum to 2048, and one of them equals 256. `response_target`: among the 10 responses of one rollout group at most 2 name the same learner device, and in some groups one device is named by exactly 2.
All inputs are finite; a program needn't handle non-finite values.
Results may differ from a plain program's by a relative error of at most 0.0065.
The roundings to bfloat16 on the way count: a program that leaves them out, or rounds other values in their place, can miss the bound.
Values may be sent and summed in bfloat16 or wider, within the bound.
A program may use at most 64 MiB of HBM per device.

v0:
```python
import math
import jax
import jax.numpy as jnp
from jax import lax
from jax.sharding import PartitionSpec as P

MODEL_WIDTH = 5120
QUERY_HEADS = 40
KV_HEADS = 8
HEAD_DIM = 128
DONE_PER_GROUP = 10
RESPONSE_LIMIT = 64


def normalize(rows_in, gain_vec):
    widened = rows_in.astype(jnp.float32)
    inverse = lax.rsqrt(jnp.mean(widened * widened, axis=-1, keepdims=True) + 1e-06)
    return (widened * inverse * gain_vec.astype(jnp.float32)).astype(jnp.bfloat16)


def block_attend(qkv_rows, token_lengths):
    rollout_groups = qkv_rows.shape[3] - 2
    head_size = qkv_rows.shape[4]
    number = qkv_rows.shape[0]
    length = qkv_rows.shape[1]
    query = qkv_rows[:, :, :, :rollout_groups]
    key_matrix = qkv_rows[:, :, :, rollout_groups]
    value_matrix = qkv_rows[:, :, :, rollout_groups + 1]
    scores = jnp.einsum(
        "nikgh,njkh->nkgij", query, key_matrix, preferred_element_type=jnp.float32
    ) / math.sqrt(head_size)
    causal = jnp.arange(length)[None, :] <= jnp.arange(length)[:, None]
    masked = jnp.where(causal, scores, -jnp.inf)
    peak = jnp.max(masked, axis=-1, keepdims=True)
    powers = jnp.where(causal, jnp.exp(scores - peak), 0.0)
    probs = (powers / jnp.sum(powers, axis=-1, keepdims=True)).astype(jnp.bfloat16)
    mixture = jnp.einsum(
        "nkgij,njkh->nikgh", probs, value_matrix, preferred_element_type=jnp.float32
    )
    in_range = jnp.arange(length)[None, :] < token_lengths[:, None]
    mixture = jnp.where(in_range[:, :, None, None, None], mixture, 0.0)
    return mixture.astype(jnp.bfloat16).reshape(number, length, -1)


def attend_decoding(qkv_rows, key_cache, value_cache, token_lengths):
    rollout_groups = qkv_rows.shape[2] - 2
    head_size = qkv_rows.shape[3]
    number = qkv_rows.shape[0]
    query = qkv_rows[:, :, :rollout_groups]
    new_key = qkv_rows[:, :, rollout_groups]
    new_value = qkv_rows[:, :, rollout_groups + 1]
    scores = jnp.einsum(
        "bkgh,bklh->bkgl", query, key_cache, preferred_element_type=jnp.float32
    ) / math.sqrt(head_size)
    self_score = jnp.einsum("bkgh,bkh->bkg", query, new_key, preferred_element_type=jnp.float32)[
        ..., None
    ] / math.sqrt(head_size)
    filled = (jnp.arange(key_cache.shape[2])[None, :] < token_lengths[:, None])[:, None, None, :]
    peak = jnp.maximum(
        jnp.max(jnp.where(filled, scores, -jnp.inf), axis=-1, keepdims=True), self_score
    )
    powers = jnp.where(filled, jnp.exp(scores - peak), 0.0)
    self_power = jnp.exp(self_score - peak)
    total = jnp.sum(powers, axis=-1, keepdims=True) + self_power
    probs = (powers / total).astype(jnp.bfloat16)
    self_prob = (self_power / total).astype(jnp.bfloat16)
    mixture = jnp.einsum("bkgl,bklh->bkgh", probs, value_cache, preferred_element_type=jnp.float32)
    mixture = mixture + self_prob.astype(jnp.float32) * new_value.astype(jnp.float32)[:, :, None, :]
    return mixture.astype(jnp.bfloat16).reshape(number, -1)


def selector(targets, shards, slot_capacity):
    number = targets.shape[0]
    same_dest = targets[:, None] == targets[None, :]
    earlier = jnp.arange(number)[None, :] < jnp.arange(number)[:, None]
    slot_index = jnp.sum((same_dest & earlier).astype(jnp.int32), axis=1)
    target_slot = targets * slot_capacity + slot_index
    return (
        jnp.arange(shards * slot_capacity, dtype=jnp.int32)[:, None] == target_slot[None, :]
    ).astype(jnp.int32)


def body(
    qkv_weight,
    qkv_bias,
    norm_gain,
    decode_hidden,
    stored_keys,
    stored_values,
    stored_lengths,
    response_hidden,
    response_lengths,
    response_target,
):
    tensor_count = lax.axis_size("tensor")
    rollout_groups = QUERY_HEADS // KV_HEADS
    slot_capacity = DONE_PER_GROUP // tensor_count + 1
    rows_local = qkv_weight.shape[0]
    col_width = qkv_weight.shape[1] // tensor_count
    local_groups = col_width // ((rollout_groups + 2) * HEAD_DIM)
    blocks = lax.all_to_all(
        qkv_weight.reshape(rows_local, tensor_count, col_width),
        "tensor",
        split_axis=1,
        concat_axis=0,
        tiled=True,
    )
    blocks = blocks.reshape(rows_local * tensor_count, col_width)
    step_norm = normalize(decode_hidden, norm_gain)
    resp_full = lax.all_gather(response_hidden, "tensor", axis=2, tiled=True)
    resp_norm = normalize(resp_full, norm_gain).reshape(
        DONE_PER_GROUP * RESPONSE_LIMIT, MODEL_WIDTH
    )
    weight_all = lax.all_gather(blocks, "replica", axis=0, tiled=True)
    step_acc = jnp.dot(step_norm, weight_all, preferred_element_type=jnp.float32)
    resp_acc = jnp.dot(resp_norm, weight_all, preferred_element_type=jnp.float32)
    offset = qkv_bias.astype(jnp.float32)
    decode_projected = (
        (step_acc + offset)
        .astype(jnp.bfloat16)
        .reshape(-1, local_groups, rollout_groups + 2, HEAD_DIM)
    )
    response_projected = (
        (resp_acc + offset).astype(jnp.bfloat16).reshape(DONE_PER_GROUP, RESPONSE_LIMIT, col_width)
    )
    decode_output = attend_decoding(
        decode_projected, stored_keys, stored_values, stored_lengths.reshape(-1)
    )
    token_lengths = response_lengths.reshape(DONE_PER_GROUP)
    targets = response_target.reshape(DONE_PER_GROUP)
    chooser = selector(targets, tensor_count, slot_capacity)
    mine = lax.dynamic_slice_in_dim(
        chooser, lax.axis_index("tensor") * slot_capacity, slot_capacity, 0
    )
    slot_lens = jnp.sum(mine * token_lengths[None, :], axis=1)
    chooser_cube = chooser.astype(jnp.bfloat16).reshape(tensor_count, slot_capacity, DONE_PER_GROUP)
    sendbuf = jnp.einsum(
        "dcj,jrw->crdw", chooser_cube, response_projected, preferred_element_type=jnp.float32
    ).astype(jnp.bfloat16)
    received_rows = lax.all_to_all(sendbuf, "tensor", split_axis=2, concat_axis=2, tiled=True)
    received_rows = received_rows.reshape(
        slot_capacity, RESPONSE_LIMIT, KV_HEADS, rollout_groups + 2, HEAD_DIM
    )
    learner_out = block_attend(received_rows, slot_lens)
    return (decode_output, learner_out)


def solution(mesh):
    return jax.shard_map(
        body,
        mesh=mesh,
        in_specs=(
            P(("replica", "tensor"), None),
            P("tensor"),
            P(),
            P("replica", None),
            P("replica", "tensor", None, None),
            P("replica", "tensor", None, None),
            P("replica", None),
            P("replica", None, "tensor"),
            P("replica", None),
            P("replica", None),
        ),
        out_specs=(P("replica", "tensor"), P(("replica", "tensor"), None, None)),
        check_vma=False,
    )
```

profile of v0, /device:TPU:1, one launch (start us, length us, event | category | flops | bytes accessed | tf_op | source)
XLA Modules:
  0.0 312.3 jit_solution(8639920904462327456)
XLA Ops:
  7.3 0.7 all-gather.5.cloned.1.call-update
  8.0 1.0 copy.58
  9.0 14.8 %all_to_all.20 = bf16[10,8,896]{2,0,1:T(8,128)(2,1)S(1)} all-to-all(bf16[10,8,896]{2,0,1:T(8,128)(2,1)S(1)} %copy.38), channel_id=1, replica_groups=mesh['replica'=64,'tensor'=8] {'tensor'}, dimensions={1} | all-to-all | bytes 286720 | tf_op jit(solution)/shard_map/all_to_all | solution.py:101
  23.8 0.7 reshape.186
  24.6 0.2 convert_reduce_fusion
  24.8 0.1 fusion.42
  25.0 0.2 fusion.22
  25.2 0.1 iota_compare_fusion.1
  25.3 96.4 %all-gather.5.cloned.1.call-done = bf16[10,64,5120]{2,1,0:T(8,128)(2,1)} async-done(((bf16[10,64,640]{2,1,0:T(8,128)(2,1)}), bf16[10,64,5120]{2,1,0:T(8,128)(2,1)}) %all-gather.5.cloned.1.call-update) | async-done | bytes 6553616 | tf_op jit(solution)/shard_map/all_gather | solution.py:110
  121.7 4.4 %fusion.1 = f32[10,64]{1,0:T(8,128)S(1)} fusion(bf16[10,64,5120]{2,1,0:T(8,128)(2,1)} %all-gather.5.cloned.1.call-done), kind=kLoop, calls=%fused_computation.3 | loop fusion | flops 9829760 | bytes 6556160 | tf_op jit(solution)/shard_map/reduce_sum | solution.py:17
  126.1 0.4 copy-done.1
  126.4 5.3 %fusion.3 = bf16[10,64,5120]{2,1,0:T(8,128)(2,1)} fusion(bf16[10,64,5120]{2,1,0:T(8,128)(2,1)S(1)} %copy-done.1, f32[5120]{0:T(1024)S(1)} %convert_element_type.82, f32[10,64]{1,0:T(8,128)S(1)} %add_rsqrt_fusion), kind=kLoop, calls=%fused_computation.5 | loop fusion | flops 13107200 | bytes 13130240 | tf_op jit(solution)/shard_map/convert_element_type | solution.py:18
  131.7 121.0 %all-gather.3.cloned.1.call-done = bf16[5120,896]{1,0:T(8,128)(2,1)} async-done(((bf16[80,896]{1,0:T(8,128)(2,1)}), bf16[5120,896]{1,0:T(8,128)(2,1)}) %all-gather.3.cloned.1.call-update) | async-done | bytes 9175056 | tf_op jit(solution)/shard_map/all_gather | solution.py:114
  252.8 11.8 %add_convert_fusion = bf16[640,896]{1,0:T(8,128)(2,1)S(1)} fusion(bf16[640,5120]{1,0:T(8,128)(2,1)} %bitcast.81, bf16[5120,896]{1,0:T(8,128)(2,1)} %all-gather.3.cloned.1.call-done, f32[896]{0:T(1024)S(1)} %convert_element_type.84), kind=kOutput, calls=%fused_computation.14 | convolution fusion | flops 5873172480 | bytes 16879104 | tf_op jit(solution)/shard_map/dot_general | solution.py:116
  264.5 0.9 convert_bitcast_fusion
  265.5 2.7 copy.40
  268.1 6.4 %all-to-all-start.1 = ((bf16[2,64,8,896]{3,0,1,2:T(2,128)(2,1)}), bf16[2,64,8,896]{3,0,1,2:T(2,128)(2,1)S(1)}, u32[]{:S(2)}, u32[]{:S(2)}) async-start(bf16[2,64,8,896]{3,0,1,2:T(2,128)(2,1)} %copy.40), calls=%async_computation.1 | async-start | bytes 3670016 | tf_op jit(solution)/shard_map/all_to_all | solution.py:140
  274.6 4.9 %fusion.19 = bf16[16,896]{1,0:T(8,128)(2,1)S(1)} fusion(bf16[5120,896]{1,0:T(8,128)(2,1)} %all-gather.3.cloned.1.call-done, bf16[16,5120]{1,0:T(8,128)(2,1)S(1)} %copy-done.2, f32[5120]{0:T(1024)S(1)} %convert_element_type.82, f32[16]{0:T(128)S(1)} %add_rsqrt_fusion.1, f32[896]{0:T(1024)S(1)} %convert_element_type.84), kind=kOutput, calls=%fused_computation.29 | convolution fusion | flops 147156992 | bytes 9391680 | tf_op jit(solution)/shard_map/dot_general | solution.py:115
  279.6 0.1 fusion.33
  279.7 0.5 select_reduce_fusion
  280.2 0.2 fusion.28
  280.4 1.5 fusion.18
  281.9 0.6 copy.73
  282.6 15.4 %all-to-all-done.1 = bf16[2,64,8,896]{3,0,1,2:T(2,128)(2,1)S(1)} async-done(((bf16[2,64,8,896]{3,0,1,2:T(2,128)(2,1)}), bf16[2,64,8,896]{3,0,1,2:T(2,128)(2,1)S(1)}, u32[]{:S(2)}, u32[]{:S(2)}) %all-to-all-start.1) | async-done | bytes 1835040 | tf_op jit(solution)/shard_map/all_to_all | solution.py:140
  298.0 1.0 copy.72
  299.0 0.1 fusion.46
  299.1 0.1 slice.29
  299.2 1.2 fusion.13
  300.4 1.0 fusion.47
  301.4 0.8 fusion.12
  302.2 0.9 copy.46
  303.2 2.3 reshape.197
  (32 shorter events, 0.4 us)
Async XLA Ops:
  7.2 272.5 %copy-start = (bf16[16,1,256,128]{3,2,1,0:T(8,128)(2,1)S(1)}, bf16[16,1,256,128]{3,2,1,0:T(8,128)(2,1)}, u32[]{:S(2)}) copy-start(bf16[16,1,256,128]{3,2,1,0:T(8,128)(2,1)} %param.14) | copy-start | bytes 3145732
  7.2 17.4 %copy-start.4 = (bf16[896]{0:T(1024)(128)(2,1)S(1)}, bf16[896]{0:T(1024)(128)(2,1)}, u32[]{:S(2)}) copy-start(bf16[896]{0:T(1024)(128)(2,1)} %param.11) | copy-start | bytes 5380
  7.2 17.4 %copy-start.3 = (bf16[5120]{0:T(1024)(128)(2,1)S(1)}, bf16[5120]{0:T(1024)(128)(2,1)}, u32[]{:S(2)}) copy-start(bf16[5120]{0:T(1024)(128)(2,1)} %param.12) | copy-start | bytes 30724
  7.2 17.4 %copy-start.7 = (s32[10,1]{0,1:T(1,128)S(1)}, s32[10,1]{0,1:T(1,128)}, u32[]{:S(2)}) copy-start(s32[10,1]{0,1:T(1,128)} %param.19) | copy-start | bytes 124
  7.2 17.6 %copy-start.6 = (s32[1,10]{1,0:T(1,128)S(1)}, s32[1,10]{1,0:T(1,128)}, u32[]{:S(2)}) copy-start(s32[1,10]{1,0:T(1,128)} %param.18) | copy-start | bytes 124
  7.2 17.7 %copy-start.2 = (bf16[16,5120]{1,0:T(8,128)(2,1)S(1)}, bf16[16,5120]{1,0:T(8,128)(2,1)}, u32[]{:S(2)}) copy-start(bf16[16,5120]{1,0:T(8,128)(2,1)} %param.13) | copy-start | bytes 491524
  7.2 18.0 %copy-start.5 = (s32[1,16]{1,0:T(1,128)S(1)}, s32[1,16]{1,0:T(1,128)}, u32[]{:S(2)}) copy-start(s32[1,16]{1,0:T(1,128)} %param.16) | copy-start | bytes 196
  7.2 114.5 %all-gather.5.cloned.1.call-start = ((), (), s32[]{:S(2)}) async-start(), calls=%async_computation.3 | async-start | bytes 7372800 | tf_op jit(solution)/shard_map/all_gather | solution.py:110
  8.0 244.8 %all-gather.3.cloned.1.call-start = ((), (), s32[]{:S(2)}) async-start(), calls=%async_computation.2 | async-start | bytes 9318400 | tf_op jit(solution)/shard_map/all_gather | solution.py:114
  121.7 4.7 %copy-start.1 = (bf16[10,64,5120]{2,1,0:T(8,128)(2,1)S(1)}, bf16[10,64,5120]{2,1,0:T(8,128)(2,1)}, u32[]{:S(2)}) copy-start(bf16[10,64,5120]{2,1,0:T(8,128)(2,1)} %all-gather.5.cloned.1.call-done) | copy-start | bytes 19660804
  268.1 29.8 %all-to-all-start.1 = ((bf16[2,64,8,896]{3,0,1,2:T(2,128)(2,1)}), bf16[2,64,8,896]{3,0,1,2:T(2,128)(2,1)S(1)}, u32[]{:S(2)}, u32[]{:S(2)}) async-start(bf16[2,64,8,896]{3,0,1,2:T(2,128)(2,1)} %copy.40), calls=%async_computation.1 | async-start | bytes 3670016 | tf_op jit(solution)/shard_map/all_to_all | solution.py:140
Sparse Core Ops, SparseCore 0:
  11.3 110.3 all-gather.4
  124.4 128.2 all-gather.2
where the time goes:
time: 313 us; the launch traced here: 312 us
  waiting for transfers between devices  234 us (75%)
  matrix products  21.8 us (7%)
  blocking collectives  14.8 us (5%)
  between operations  14.3 us (5%)
  other arithmetic  11.5 us (4%)
  local copies, waits for them, and re-layouts  9.97 us (3%)
  starting transfers between devices  6.51 us (2%)
    all_gather x1, waiting for transfers between devices, body(): weight_all = lax.all_gather(blocks, 'replica', axis=0, tiled=True)  121 us
    all_gather x1, waiting for transfers between devices, body(): resp_full = lax.all_gather(response_hidden, 'tensor', axis=2, tiled=True)  96.4 us
    all_to_all x1, waiting for transfers between devices, body(): lax.all_to_all(sendbuf, 'tensor', split_axis=2, concat_axis=2, tiled=True)  15.4 us
    all_to_all x1, blocking collectives, body(): lax.all_to_all(qkv_weight.reshape(rows_local, tensor_count, col_width), '...  14.8 us
    dot_general x1, matrix products, body(): jnp.dot(resp_norm, weight_all, preferred_element_type=jnp.float32)  11.8 us
    all_to_all x1, starting transfers between devices, body(): lax.all_to_all(sendbuf, 'tensor', split_axis=2, concat_axis=2, tiled=True)  6.43 us
  transfers between devices with their start and end apart: 3, of which 3 were waited for; matrix products, arithmetic and copies ran while one was open for 6% of the time, Pallas kernels for 0%

commit v1 on v0

--- a/solution.py
+++ b/solution.py
@@ -107,7 +107,10 @@
     )
     blocks = blocks.reshape(rows_local * tensor_count, col_width)
     step_norm = normalize(decode_hidden, norm_gain)
-    resp_full = lax.all_gather(response_hidden, "tensor", axis=2, tiled=True)
+    resp_full = jnp.concatenate(
+        lax.all_to_all(jnp.stack([response_hidden] * lax.axis_size("tensor")), "tensor", 0, 0),
+        axis=2,
+    )
     resp_norm = normalize(resp_full, norm_gain).reshape(
         DONE_PER_GROUP * RESPONSE_LIMIT, MODEL_WIDTH
     )

time: 313 us -> 254 us (0.81)
  the two profiles are of different devices: /device:TPU:1 before, /device:TPU:480 now
where the time goes in v1:
time: 254 us
  waiting for transfers between devices  133 us (52%)
  local copies, waits for them, and re-layouts  43.6 us (17%)
  matrix products  22.8 us (9%)
  other arithmetic  15.5 us (6%)
  blocking collectives  15.3 us (6%)
  between operations  14.3 us (6%)
  starting transfers between devices  9.3 us (4%)
    all_to_all x1, waiting for transfers between devices, body(): lax.all_to_all(jnp.stack([response_hidden] * lax.axis_size('tensor')), 't...  120 us
    convert_element_type x1, local copies, waits for them, and re-layouts, normalize(): widened = rows_in.astype(jnp.float32)  17.6 us
    all_to_all x1, blocking collectives, body(): lax.all_to_all(qkv_weight.reshape(rows_local, tensor_count, col_width), '...  15.3 us
    unnamed x19, local copies, waits for them, and re-layouts  14.3 us
    all_to_all x1, waiting for transfers between devices, body(): lax.all_to_all(sendbuf, 'tensor', split_axis=2, concat_axis=2, tiled=True)  13.2 us
    dot_general x1, matrix products, body(): jnp.dot(resp_norm, weight_all, preferred_element_type=jnp.float32)  12.8 us
    convert_element_type x1, other arithmetic, normalize(): widened = rows_in.astype(jnp.float32)  9.4 us
  transfers between devices with their start and end apart: 3, of which 2 were waited for; matrix products, arithmetic and copies ran while one was open for 22% of the time, Pallas kernels for 0%

profile of v1, /device:TPU:480, one launch (start us, length us, event | category | flops | bytes accessed | tf_op | source)
XLA Modules:
  0.0 253.8 jit_solution(7076216400532743673)
XLA Ops:
  7.2 1.1 copy.61
  8.4 15.3 %all_to_all.25 = bf16[10,8,896]{2,0,1:T(8,128)(2,1)S(1)} all-to-all(bf16[10,8,896]{2,0,1:T(8,128)(2,1)S(1)} %copy.40), channel_id=1, replica_groups=mesh['replica'=64,'tensor'=8] {'tensor'}, dimensions={1} | all-to-all | bytes 286720 | tf_op jit(solution)/shard_map/all_to_all | solution.py:101
  23.7 0.7 reshape.199
  24.5 3.7 %stack.2 = bf16[8,10,64,640]{3,2,1,0:T(8,128)(2,1)} broadcast(bf16[10,64,640]{2,1,0:T(8,128)(2,1)S(1)} %copy-done.2), dimensions={1,2,3} | broadcast | bytes 7372800 | tf_op jit(solution)/shard_map/stack | solution.py:111
  28.2 5.0 %all-to-all-start.1 = ((bf16[8,10,64,640]{3,2,1,0:T(8,128)(2,1)}), bf16[8,10,64,640]{3,2,1,0:T(8,128)(2,1)}, u32[]{:S(2)}, u32[]{:S(2)}) async-start(bf16[8,10,64,640]{3,2,1,0:T(8,128)(2,1)} %stack.2), calls=%async_computation.1 | async-start | bytes 13107200 | tf_op jit(solution)/shard_map/all_to_all | solution.py:111
  33.3 0.2 convert_reduce_fusion
  33.5 0.1 fusion.43
  33.6 0.2 fusion.23
  33.9 119.8 %all-to-all-done.1 = bf16[8,10,64,640]{3,2,1,0:T(8,128)(2,1)} async-done(((bf16[8,10,64,640]{3,2,1,0:T(8,128)(2,1)}), bf16[8,10,64,640]{3,2,1,0:T(8,128)(2,1)}, u32[]{:S(2)}, u32[]{:S(2)}) %all-to-all-start.1) | async-done | bytes 6553632 | tf_op jit(solution)/shard_map/all_to_all | solution.py:111
  153.7 4.2 %fusion.1 = f32[10,64]{1,0:T(8,128)S(1)} fusion(bf16[8,10,64,640]{3,2,1,0:T(8,128)(2,1)} %all-to-all-done.1), kind=kLoop, calls=%fused_computation.3 | loop fusion | flops 9829760 | bytes 6556160 | tf_op jit(solution)/shard_map/reduce_sum | solution.py:17
  158.0 9.4 %convert_bitcast_fusion = f32[10,64,8,640]{3,1,0,2:T(8,128)} fusion(bf16[8,10,64,640]{3,2,1,0:T(8,128)(2,1)} %all-to-all-done.1), kind=kLoop, calls=%fused_computation.2 | loop fusion | flops 3276800 | bytes 19660800 | tf_op jit(solution)/shard_map/convert_element_type | solution.py:16
  167.4 17.6 %copy.41 = f32[10,64,8,640]{3,2,1,0:T(8,128)} copy(f32[10,64,8,640]{3,1,0,2:T(8,128)} %convert_bitcast_fusion) | data formatting | bytes 26214400 | tf_op jit(solution)/shard_map/convert_element_type | solution.py:16
  185.0 12.5 %copy.63 = f32[80,8,8,640]{3,1,2,0:T(8,128)} copy(f32[80,8,8,640]{3,2,1,0:T(8,128)} %bitcast.82) | data formatting | bytes 26214400
  197.5 12.8 %add_convert_fusion = bf16[640,896]{1,0:T(8,128)(2,1)S(1)} fusion(bf16[5120,896]{1,0:T(8,128)(2,1)} %all-gather.2.cloned.1.call-done, f32[640,5120]{1,0:T(8,128)} %bitcast.83, f32[5120]{0:T(1024)S(1)} %convert_element_type.94, f32[640]{0:T(1024)S(1)} %rsqrt.21, f32[896]{0:T(1024)S(1)} %convert_element_type.96), kind=kOutput, calls=%fused_computation.16 | convolution fusion | flops 5883002880 | bytes 23455744 | tf_op jit(solution)/shard_map/dot_general | solution.py:119
  210.3 0.9 convert_bitcast_fusion.1
  211.3 2.7 %copy.43 = bf16[2,64,8,896]{3,0,1,2:T(2,128)(2,1)} copy(bf16[2,64,8,896]{3,2,0,1:T(8,128)(2,1)S(1)} %convert_bitcast_fusion.1) | data formatting | bytes 3670016 | tf_op jit(solution)/shard_map/convert_element_type | solution.py:142
  213.9 4.3 %all-to-all-start.2 = ((bf16[2,64,8,896]{3,0,1,2:T(2,128)(2,1)}), bf16[2,64,8,896]{3,0,1,2:T(2,128)(2,1)S(1)}, u32[]{:S(2)}, u32[]{:S(2)}) async-start(bf16[2,64,8,896]{3,0,1,2:T(2,128)(2,1)} %copy.43), calls=%async_computation.2 | async-start | bytes 3670016 | tf_op jit(solution)/shard_map/all_to_all | solution.py:143
  218.2 4.9 %fusion.20 = bf16[16,896]{1,0:T(8,128)(2,1)S(1)} fusion(bf16[5120,896]{1,0:T(8,128)(2,1)} %all-gather.2.cloned.1.call-done, bf16[16,5120]{1,0:T(8,128)(2,1)S(1)} %copy-done.1, f32[5120]{0:T(1024)S(1)} %convert_element_type.94, f32[16]{0:T(128)S(1)} %add_rsqrt_fusion.1, f32[896]{0:T(1024)S(1)} %convert_element_type.96), kind=kOutput, calls=%fused_computation.31 | convolution fusion | flops 147156992 | bytes 9391680 | tf_op jit(solution)/shard_map/dot_general | solution.py:118
  223.2 0.1 fusion.34
  223.4 0.5 select_reduce_fusion
  223.9 0.2 fusion.29
  224.1 1.5 fusion.19
  225.6 0.6 copy.77
  226.2 13.2 %all-to-all-done.2 = bf16[2,64,8,896]{3,0,1,2:T(2,128)(2,1)S(1)} async-done(((bf16[2,64,8,896]{3,0,1,2:T(2,128)(2,1)}), bf16[2,64,8,896]{3,0,1,2:T(2,128)(2,1)S(1)}, u32[]{:S(2)}, u32[]{:S(2)}) %all-to-all-start.2) | async-done | bytes 1835040 | tf_op jit(solution)/shard_map/all_to_all | solution.py:143
  239.5 1.0 copy.76
  240.5 0.1 fusion.47
  240.6 0.1 slice.29
  240.7 1.2 fusion.14
  241.9 1.0 fusion.48
  242.9 0.8 fusion.13
  243.7 0.9 copy.49
  244.7 2.3 reshape.209
  (35 shorter events, 0.5 us)
Async XLA Ops:
  7.2 216.2 %copy-start = (bf16[16,1,256,128]{3,2,1,0:T(8,128)(2,1)S(1)}, bf16[16,1,256,128]{3,2,1,0:T(8,128)(2,1)}, u32[]{:S(2)}) copy-start(bf16[16,1,256,128]{3,2,1,0:T(8,128)(2,1)} %param.14) | copy-start | bytes 3145732
  7.2 17.3 %copy-start.2 = (bf16[10,64,640]{2,1,0:T(8,128)(2,1)S(1)}, bf16[10,64,640]{2,1,0:T(8,128)(2,1)}, u32[]{:S(2)}) copy-start(bf16[10,64,640]{2,1,0:T(8,128)(2,1)} %param.17) | copy-start | bytes 2457604
  7.2 190.3 %all-gather.2.cloned.1.call-start = ((), (), s32[]{:S(2)}) async-start(), calls=%async_computation.3 | async-start | bytes 9318400 | tf_op jit(solution)/shard_map/all_gather | solution.py:117
  28.2 5.0 %copy-start.4 = (bf16[896]{0:T(1024)(128)(2,1)S(1)}, bf16[896]{0:T(1024)(128)(2,1)}, u32[]{:S(2)}) copy-start(bf16[896]{0:T(1024)(128)(2,1)} %param.11) | copy-start | bytes 5380
  28.2 5.0 %copy-start.3 = (bf16[5120]{0:T(1024)(128)(2,1)S(1)}, bf16[5120]{0:T(1024)(128)(2,1)}, u32[]{:S(2)}) copy-start(bf16[5120]{0:T(1024)(128)(2,1)} %param.12) | copy-start | bytes 30724
  28.2 5.1 %copy-start.7 = (s32[10,1]{0,1:T(1,128)S(1)}, s32[10,1]{0,1:T(1,128)}, u32[]{:S(2)}) copy-start(s32[10,1]{0,1:T(1,128)} %param.19) | copy-start | bytes 124
  28.2 5.3 %copy-start.6 = (s32[1,10]{1,0:T(1,128)S(1)}, s32[1,10]{1,0:T(1,128)}, u32[]{:S(2)}) copy-start(s32[1,10]{1,0:T(1,128)} %param.18) | copy-start | bytes 124
  28.2 5.4 %copy-start.1 = (bf16[16,5120]{1,0:T(8,128)(2,1)S(1)}, bf16[16,5120]{1,0:T(8,128)(2,1)}, u32[]{:S(2)}) copy-start(bf16[16,5120]{1,0:T(8,128)(2,1)} %param.13) | copy-start | bytes 491524
  28.2 5.6 %copy-start.5 = (s32[1,16]{1,0:T(1,128)S(1)}, s32[1,16]{1,0:T(1,128)}, u32[]{:S(2)}) copy-start(s32[1,16]{1,0:T(1,128)} %param.16) | copy-start | bytes 196
  28.2 125.5 %all-to-all-start.1 = ((bf16[8,10,64,640]{3,2,1,0:T(8,128)(2,1)}), bf16[8,10,64,640]{3,2,1,0:T(8,128)(2,1)}, u32[]{:S(2)}, u32[]{:S(2)}) async-start(bf16[8,10,64,640]{3,2,1,0:T(8,128)(2,1)} %stack.2), calls=%async_computation.1 | async-start | bytes 13107200 | tf_op jit(solution)/shard_map/all_to_all | solution.py:111
  213.9 25.5 %all-to-all-start.2 = ((bf16[2,64,8,896]{3,0,1,2:T(2,128)(2,1)}), bf16[2,64,8,896]{3,0,1,2:T(2,128)(2,1)S(1)}, u32[]{:S(2)}, u32[]{:S(2)}) async-start(bf16[2,64,8,896]{3,0,1,2:T(2,128)(2,1)} %copy.43), calls=%async_computation.2 | async-start | bytes 3670016 | tf_op jit(solution)/shard_map/all_to_all | solution.py:143
Sparse Core Ops, SparseCore 0:
  24.6 121.5 all-gather.1
